TPU v7x, 32 devices: a whole 2x2x4 slice. The times are simulated.
32 devices in a mesh: gx: 4 (over z), gy: 2 (over x), gz: 4 (over y, core).
Axes of the slice: x: 2, y: 2, z: 4, core: 2. Of those that a mesh axis runs over, the one named last changes fastest.
Arguments:
- tri_geom: float32 [10, 32768], P(None, ('gx', 'gy', 'gz')), as said below
- send_index: int32 [256, 128], P(('gx', 'gy', 'gz')), may hold values from -1 to 1023, as said below
- near_index: int32 [32, 64, 512], P('gx', 'gy', 'gz'), may hold values from 0 to 1023, as said below
- return_cell: int32 [3, 32768], P(None, ('gx', 'gy', 'gz')), may hold values from -1 to 32767, as said below
- velocity: float32 [3, 32, 64, 512], P(None, 'gx', 'gy', 'gz'), may hold values from -6 to 6
Outputs:
- new_velocity: float32 [3, 32, 64, 512], P(None, 'gx', 'gy', 'gz')
- indicator: float32 [32, 64, 512], P('gx', 'gy', 'gz')
- vertex_velocity: float32 [9, 32768], P(None, ('gx', 'gy', 'gz'))
Inputs may be any that keep to these rules, and one draw needn't show every extreme that they name: `send_index`: each row lists distinct local triangle indices of its owner in its first entries and -1 in the rest; every row has at least one triangle; an owner lists each of its triangles at most once over all its rows; for some bricks every owner fills all 128 slots. `near_index`: A value j * 128 + k names a slot that holds a triangle: k is below the number of triangles that owner j of the cell's row along gz lists for the cell's brick. `return_cell`: -1 where the vertex lies outside the brick. `tri_geom`: row 9 lies between 0.25 and 3.
All inputs are finite; a program needn't handle non-finite values.
Results may differ from a plain program's by a relative error of at most 0.0003.
Values sent between devices are 32-bit elements; how exact they have to be, the bound alone decides.
A program may use at most 128 MiB of HBM per device.

v0:
```python
import jax
import jax.numpy as jnp
from jax import lax
from jax.experimental import pallas as pl
from jax.experimental.pallas import tpu as pltpu
from jax.sharding import PartitionSpec as P

CAP = 128
NSWEEP = 4
LANES = 128


time_step = 0.04
smear_width = 4.0
rho_liquid = 1.0
rho_gas = 0.05
mu_liquid = 2.0
mu_gas = 0.2


def loop(count, body, init):
    if count <= 8:
        for i in range(count):
            init = body(i, init)
        return init
    return lax.fori_loop(0, count, body, init)


def span(low, high, step, body, init):
    turns = (high - low) // step
    if turns > 1:

        def turn(i, carry):
            for k in range(step):
                carry = body(low + i * step + k, carry)
            return carry

        init = lax.fori_loop(0, turns, turn, init)
        low += turns * step
    for x in range(low, high):
        init = body(x, init)
    return init


UN_NEAR, UN_SWEEP, UN_FIRST, UN_FORCE, UN_INV = 2, 3, 4, 4, 4


def lane_pick(source, lane):
    return jnp.take_along_axis(source, lane, axis=1, mode="promise_in_bounds")


def build_table(tri_ref, table_ref):
    for t in range(table_ref.shape[0]):
        here = slice(t * LANES, (t + 1) * LANES)
        row = [tri_ref[i : i + 1, here] for i in range(10)]
        ax, ay, az = row[3] - row[0], row[4] - row[1], row[5] - row[2]
        bx, by, bz = row[6] - row[0], row[7] - row[1], row[8] - row[2]
        nx = ay * bz - az * by
        ny = az * bx - ax * bz
        nz = ax * by - ay * bx
        scale = jnp.maximum(jnp.sqrt(nx * nx + ny * ny + nz * nz), 1.0)
        table_ref[t, 0:1] = nx / scale
        table_ref[t, 1:2] = ny / scale
        table_ref[t, 2:3] = nz / scale
        for i in range(3):
            table_ref[t, 3 + i : 4 + i] = (row[i] + row[3 + i] + row[6 + i]) / 3.0
        table_ref[t, 6:7] = row[9]
        table_ref[t, 7:8] = row[9]


def pick_outgoing(send_ref, table_ref, out_ref):
    def each(d, carry):
        index = jnp.broadcast_to(send_ref[pl.ds(d, 1), :], (8, LANES))
        lane, tile = index & (LANES - 1), index >> 7

        def inner(t, found):
            return jnp.where(tile == t, lane_pick(table_ref[t], lane), found)

        out_ref[d] = loop(table_ref.shape[0], inner, jnp.zeros((8, LANES), jnp.float32))
        return carry

    loop(send_ref.shape[0], each, 0)


def local_table(arrived_ref, tab_ref, origin):
    nx, ny, nz = (arrived_ref[:, i, :] for i in range(3))
    offset = nx * (origin[0] - arrived_ref[:, 3, :])
    offset = offset + ny * (origin[1] - arrived_ref[:, 4, :])
    offset = offset + nz * (origin[2] - arrived_ref[:, 5, :])
    tab_ref[0], tab_ref[1], tab_ref[2] = nx, ny, nz
    tab_ref[3] = offset
    tab_ref[4] = arrived_ref[:, 6, :]


def iota(shape, axis):
    return lax.broadcasted_iota(jnp.int32, shape, axis)


def pack_lanes(plane, p, packed):
    here = iota(plane.shape, 1) == p
    low = jnp.where(here, pltpu.roll(plane, p, 1), packed[0])
    high = jnp.where(here, pltpu.roll(plane, p + 1, 1), packed[1])
    return (low, high)


def pack_rows(plane, c, x, row_ref):
    last = plane.shape[0] - 1
    row_ref[0, c, pl.ds(x, 1), :] = plane[0:1]
    row_ref[1, c, pl.ds(x, 1), :] = plane[last : last + 1]


def around(field_ref, row_ref, lane_ref, c, x, p):
    size_y, size_z = field_ref.shape[2:]
    row, lane = iota((size_y, size_z), 0), iota((size_y, size_z), 1)
    mid = field_ref[c, x + 1]
    low_y = jnp.where(
        row == 0,
        jnp.broadcast_to(row_ref[0, c, pl.ds(x, 1), :], mid.shape),
        pltpu.roll(mid, 1, 0),
    )
    high_y = jnp.where(
        row == size_y - 1,
        jnp.broadcast_to(row_ref[1, c, pl.ds(x, 1), :], mid.shape),
        pltpu.roll(mid, size_y - 1, 0),
    )
    low_z = jnp.where(
        lane == 0, pltpu.roll(lane_ref[0], (size_z - p) % size_z, 1), pltpu.roll(mid, 1, 1)
    )
    high_z = jnp.where(
        lane == size_z - 1,
        pltpu.roll(lane_ref[1], size_z - 1 - p, 1),
        pltpu.roll(mid, size_z - 1, 1),
    )
    return mid, field_ref[c, x], field_ref[c, x + 2], low_y, high_y, low_z, high_z


def nearest(tab_ref, near_ref, ind_ref, ten_ref, row_ref, lane_ref):
    size_x, size_y, size_z = near_ref.shape
    pos_y = iota((size_y, size_z), 0).astype(jnp.float32) + 0.5
    pos_z = iota((size_y, size_z), 1).astype(jnp.float32) + 0.5
    zero = jnp.zeros((size_y, size_z), jnp.float32)

    def plane(x, packed):
        index = near_ref[x]
        lane, owner = index & (LANES - 1), index >> 7

        def inner(j, found):
            here = owner == j
            return tuple(
                jnp.where(
                    here,
                    lane_pick(
                        jnp.broadcast_to(tab_ref[f, pl.ds(j, 1), :], (size_y, size_z)), lane
                    ),
                    found[f],
                )
                for f in range(5)
            )

        nx, ny, nz, offset, tension = loop(tab_ref.shape[1], inner, (zero,) * 5)
        pos_x = jnp.asarray(x).astype(jnp.float32) + 0.5
        distance = nx * pos_x + ny * pos_y + nz * pos_z + offset
        indicator = 0.5 * (1.0 + jnp.tanh(distance / smear_width))
        ind_ref[0, x + 1] = indicator
        ten_ref[x] = tension
        pack_rows(indicator, 0, x, row_ref)
        return pack_lanes(indicator, x, packed)

    packed = span(0, size_x, UN_NEAR, plane, (zero, zero))
    lane_ref[0], lane_ref[1] = packed


def material(ind_ref, ten_ref, diff_ref):
    def plane(x, carry):
        indicator = ind_ref[0, x + 1]
        density = rho_liquid + (rho_gas - rho_liquid) * indicator
        viscosity = mu_liquid + (mu_gas - mu_liquid) * indicator
        share = time_step / density
        diff_ref[x] = viscosity * share
        ten_ref[x] = ten_ref[x] * (0.5 * share)
        return carry

    span(0, ten_ref.shape[0], UN_FORCE, plane, 0)


def forces(ind_ref, row_ref, lane_ref, ten_ref, force_ref):
    def plane(x, carry):
        near = around(ind_ref, row_ref, lane_ref, 0, x, x)
        for a in range(3):
            force_ref[a, x] = ten_ref[x] * (near[2 * a + 2] - near[2 * a + 1])
        return carry

    span(0, ten_ref.shape[0], UN_FORCE, plane, 0)


def advance(old_ref, row_ref, lane_ref, diff_ref, force_ref, new_ref, x, packed, new_rows):
    size_x = diff_ref.shape[0]
    diffusion = diff_ref[x]
    for c in range(3):
        p = c * size_x + x
        mid, *near = around(old_ref, row_ref, lane_ref, c, x, p)
        laplace = near[0] + near[1] + near[2] + near[3] + near[4] + near[5] - 6.0 * mid
        new = mid + (diffusion * laplace + force_ref[c, x])
        new_ref[c, x + 1] = new
        if new_rows is not None:
            pack_rows(new, c, x, new_rows)
            packed = pack_lanes(new, p, packed)
    return packed


def row_onehot(cell_ref, hot_ref):
    rows, slots = hot_ref.shape[1:]

    def each(i, carry):
        here = pl.ds(pl.multiple_of(i * LANES, LANES), LANES)
        for v in range(3):
            row = jnp.broadcast_to(cell_ref[v : v + 1, here] >> 7, (rows, LANES))
            hit = iota((rows, LANES), 0) == row
            hot_ref[v, :, here] = jnp.where(hit, 1.0, 0.0).astype(jnp.bfloat16)
        return carry

    lax.fori_loop(0, slots // LANES, each, 0)


def sample_field(vel_ref, cell_ref, hot_ref, out_ref, send):
    rows, slots = hot_ref.shape[1:]
    size_x = vel_ref.shape[1] - 2
    parts = [vel_ref[c, 1 : size_x + 1].reshape(rows, LANES).T for c in range(3)]
    field = jnp.concatenate(parts, axis=0)
    high = field.astype(jnp.bfloat16)
    low = (field - high.astype(jnp.float32)).astype(jnp.bfloat16)
    width = 256

    def each(i, carry):
        here = pl.ds(pl.multiple_of(i * width, width), width)
        for v in range(3):
            hot = hot_ref[v, :, here]
            got = jnp.dot(high, hot, preferred_element_type=jnp.float32)
            got = got + jnp.dot(low, hot, preferred_element_type=jnp.float32)
            lane = jnp.broadcast_to(cell_ref[v : v + 1, here] & (LANES - 1), (LANES, width))
            hit = iota((LANES, width), 0) == lane
            for c in range(3):
                picked = jnp.where(hit, got[c * LANES : (c + 1) * LANES], 0.0)
                total = jnp.sum(picked, axis=0, keepdims=True)
                for k in range(width // LANES):
                    out_ref[i * (width // LANES) + k, 3 * c + v : 3 * c + v + 1] = total[
                        :, k * LANES : (k + 1) * LANES
                    ]
        for k in range(width // LANES):
            send(i * (width // LANES) + k)
        return carry

    lax.fori_loop(0, slots // width, each, 0)


def invert(send_ref, inv_ref):
    tiles = inv_ref.shape[0]
    lane = iota((LANES, LANES), 1)
    place = iota((LANES, LANES), 0)
    inv_ref[...] = jnp.full(inv_ref.shape, -1, jnp.int32)

    def each(d, carry):
        listed = jnp.broadcast_to(send_ref[pl.ds(d, 1), :], (LANES, LANES)).T
        slot = place + (d * LANES + 1)

        def inner(t, carry):
            hit = jnp.where(listed - t * LANES == lane, slot, 0)
            inv_ref[pl.ds(t, 1), :] += jnp.sum(hit, axis=0, keepdims=True)
            return carry

        loop(tiles, inner, 0)
        return carry

    span(0, send_ref.shape[0], UN_INV if send_ref.shape[0] <= 8 else 1, each, 0)


def place_back(inv_ref, back_ref, out_ref):
    tall = back_ref.shape[1]

    def each(t, carry):
        index = jnp.broadcast_to(inv_ref[pl.ds(t, 1), :], (tall, LANES))
        lane, dest = index & (LANES - 1), index >> 7

        def inner(d, found):
            return jnp.where(dest == d, lane_pick(back_ref[d], lane), found)

        found = loop(back_ref.shape[0], inner, jnp.zeros((tall, LANES), jnp.float32))
        start = t * LANES if isinstance(t, int) else pl.multiple_of(t * LANES, LANES)
        out_ref[:, pl.ds(start, LANES)] = found[:9]
        return carry

    loop(inv_ref.shape[0], each, 0)


def f32(*shape):
    return jax.ShapeDtypeStruct(shape, jnp.float32)


AXES = ("gx", "gy", "gz")


def flow_kernel(
    tri_hbm,
    send_hbm,
    near_hbm,
    cell_hbm,
    vel_hbm,
    vel_out,
    ind_out,
    back_out,
    inv_out,
    tri_ref,
    send_ref,
    near_ref,
    cell_ref,
    table_ref,
    out_ref,
    arrived_ref,
    tab_ref,
    ind_ref,
    ten_ref,
    diff_ref,
    force_ref,
    state_ref,
    ind_rows,
    ind_lanes,
    ind_row_halo,
    ind_lane_halo,
    rows_ref,
    lanes_ref,
    row_halo,
    lane_halo,
    hot_ref,
    inv_ref,
    sample_ref,
    back_ref,
    in_sem,
    out_sem,
    there_send,
    there_recv,
    back_send,
    back_recv,
    face_send,
    face_recv,
):
    size = {a: lax.axis_size(a) for a in AXES}
    at = {a: lax.axis_index(a) for a in AXES}
    count = size["gx"] * size["gy"]
    me = at["gx"] * size["gy"] + at["gy"]
    extent = near_ref.shape
    size_x = extent[0]

    def other(d):
        return {"gx": d // size["gy"], "gy": d % size["gy"]}

    def beside(axis, step):
        return {axis: (at[axis] + step + size[axis]) % size[axis]}

    def peers(body):
        if count <= 8:
            for r in range(1, count):
                body((me + r) % count)
        else:
            pl.loop(1, count)(lambda r: body((me + r) % count))

    loads = [
        pltpu.make_async_copy(src, dst, in_sem.at[i])
        for i, (src, dst) in enumerate(
            (
                (tri_hbm, tri_ref),
                (send_hbm, send_ref),
                (vel_hbm, state_ref.at[0, :, 1 : size_x + 1]),
                (near_hbm, near_ref),
                (cell_hbm, cell_ref),
            )
        )
    ]
    for load in loads:
        load.start()
    barrier = pltpu.get_barrier_semaphore()

    def greet(device):
        pl.semaphore_signal(
            barrier, inc=1, device_id=device, device_id_type=pl.DeviceIdType.MESH
        )

    peers(lambda d: greet(other(d)))
    greet(beside("gz", 1))
    greet(beside("gz", -1))

    def remote(src, dst, send_sem, recv_sem, device):
        return pltpu.make_async_remote_copy(
            src_ref=src,
            dst_ref=dst,
            send_sem=send_sem,
            recv_sem=recv_sem,
            device_id=device,
            device_id_type=pl.DeviceIdType.MESH,
        )

    def faces(n, field, rows, lanes, halo_rows, halo_lanes):
        pairs = (
            ("gx", 1, field.at[:, size_x], field.at[:, 0]),
            ("gx", -1, field.at[:, 1], field.at[:, size_x + 1]),
            ("gy", 1, rows.at[1], halo_rows.at[0]),
            ("gy", -1, rows.at[0], halo_rows.at[1]),
            ("gz", 1, lanes.at[1], halo_lanes.at[0]),
            ("gz", -1, lanes.at[0], halo_lanes.at[1]),
        )
        return [
            remote(src, dst, face_send.at[n, i], face_recv.at[n, i], beside(axis, step))
            for i, (axis, step, src, dst) in enumerate(pairs)
        ]

    rounds = [
        faces(
            n,
            state_ref.at[n],
            rows_ref.at[n],
            lanes_ref.at[n],
            row_halo.at[n],
            lane_halo.at[n],
        )
        for n in range(NSWEEP)
    ]
    ind_round = faces(NSWEEP, ind_ref, ind_rows, ind_lanes, ind_row_halo, ind_lane_halo)

    def there(src, dst):
        return remote(
            out_ref.at[dst], arrived_ref.at[src], there_send.at[dst], there_recv.at[src], other(dst)
        )

    def back(src, dst):
        return remote(
            sample_ref.at[dst], back_ref.at[src], back_send.at[dst], back_recv.at[src], other(dst)
        )

    loads[0].wait()
    loads[1].wait()
    build_table(tri_ref, table_ref)
    pick_outgoing(send_ref, table_ref, out_ref)
    pl.semaphore_wait(barrier, count + 1)
    peers(lambda d: there(me, d).start())
    arrived_ref[me] = out_ref[me]

    loads[2].wait()
    for copy in rounds[0][:2]:
        copy.start()
    zero = jnp.zeros(extent[1:], jnp.float32)

    def first_faces(x, packed):
        for c in range(3):
            plane = state_ref[0, c, x + 1]
            pack_rows(plane, c, x, rows_ref.at[0])
            packed = pack_lanes(plane, c * size_x + x, packed)
        return packed

    packed = span(0, size_x, UN_FIRST, first_faces, (zero, zero))
    lanes_ref[0, 0], lanes_ref[0, 1] = packed
    for copy in rounds[0][2:]:
        copy.start()
    loads[4].wait()
    row_onehot(cell_ref, hot_ref)
    invert(send_ref, inv_ref)
    put_inv = pltpu.make_async_copy(inv_ref, inv_out, out_sem.at[3])
    put_inv.start()
    loads[3].wait()
    peers(lambda d: there(d, me).wait_recv())
    origin = [(at[a] * n).astype(jnp.float32) for a, n in zip(AXES, extent)]
    local_table(arrived_ref, tab_ref, origin)
    nearest(tab_ref, near_ref, ind_ref, ten_ref, ind_rows, ind_lanes)
    for copy in ind_round:
        copy.start()
    put_ind = pltpu.make_async_copy(ind_ref.at[0, 1 : size_x + 1], ind_out, out_sem.at[0])
    put_ind.start()
    material(ind_ref, ten_ref, diff_ref)
    for copy in ind_round:
        copy.wait_recv()
    forces(ind_ref, ind_row_halo, ind_lane_halo, ten_ref, force_ref)

    for n in range(NSWEEP):
        last = n == NSWEEP - 1
        for copy in rounds[n]:
            copy.wait_recv()

        def plane(x, packed):
            return advance(
                state_ref.at[n],
                row_halo.at[n],
                lane_halo.at[n],
                diff_ref,
                force_ref,
                state_ref.at[n + 1],
                x,
                packed,
                None if last else rows_ref.at[n + 1],
            )

        packed = plane(size_x - 1, plane(0, (zero, zero)))
        if not last:
            for copy in rounds[n + 1][:2]:
                copy.start()
        packed = span(1, size_x - 1, UN_SWEEP, plane, packed)
        if not last:
            lanes_ref[n + 1, 0], lanes_ref[n + 1, 1] = packed
            for copy in rounds[n + 1][2:]:
                copy.start()
    put_vel = pltpu.make_async_copy(
        state_ref.at[NSWEEP, :, 1 : size_x + 1], vel_out, out_sem.at[1]
    )
    put_vel.start()

    def send_back(d):
        @pl.when(d != me)
        def _():
            back(me, d).start()

    sample_field(state_ref.at[NSWEEP], cell_ref, hot_ref, sample_ref, send_back)
    back_ref[me] = sample_ref[me]
    peers(lambda d: back(d, me).wait_recv())
    put_back = pltpu.make_async_copy(back_ref, back_out, out_sem.at[2])
    put_back.start()
    peers(lambda d: there(me, d).wait_send())
    peers(lambda d: back(me, d).wait_send())
    for group in (ind_round, *rounds):
        for copy in group:
            copy.wait_send()
    put_ind.wait()
    put_vel.wait()
    put_back.wait()
    put_inv.wait()


def finish_kernel(
    vel_hbm, ind_hbm, back_ref, inv_ref, vel_out, ind_out, vert_out, vert_ref, sem
):
    give = [
        pltpu.make_async_copy(vel_hbm, vel_out, sem.at[0]),
        pltpu.make_async_copy(ind_hbm, ind_out, sem.at[1]),
        pltpu.make_async_copy(vert_ref, vert_out, sem.at[2]),
    ]
    give[0].start()
    give[1].start()
    place_back(inv_ref, back_ref, vert_ref)
    give[2].start()
    for copy in give:
        copy.wait()


def per_device(tri_geom, send_index, near_index, return_cell, velocity):
    count = lax.axis_size("gx") * lax.axis_size("gy")
    tri_dev = tri_geom.shape[1]
    tiles = tri_dev // LANES
    size_x, size_y, size_z = near_index.shape
    slots = return_cell.shape[1]

    def vm(*shape):
        return pltpu.VMEM(shape, jnp.float32)

    dma = pltpu.SemaphoreType.DMA
    anywhere = pl.BlockSpec(memory_space=pl.ANY)
    left = pl.pallas_call(
        flow_kernel,
        out_shape=(
            f32(*velocity.shape),
            f32(*near_index.shape),
            f32(count, 16, LANES),
            jax.ShapeDtypeStruct((tiles, LANES), jnp.int32),
        ),
        in_specs=[anywhere] * 5,
        out_specs=(anywhere,) * 4,
        scratch_shapes=[
            vm(*tri_geom.shape),
            pltpu.VMEM(send_index.shape, jnp.int32),
            pltpu.VMEM(near_index.shape, jnp.int32),
            pltpu.VMEM(return_cell.shape, jnp.int32),
            vm(tiles, 8, LANES),
            vm(count, 8, LANES),
            vm(count, 8, LANES),
            vm(5, count, LANES),
            vm(1, size_x + 2, size_y, size_z),
            vm(size_x, size_y, size_z),
            vm(size_x, size_y, size_z),
            vm(3, size_x, size_y, size_z),
            vm(NSWEEP + 1, 3, size_x + 2, size_y, size_z),
            vm(2, 1, size_x, size_z),
            vm(2, size_y, size_z),
            vm(2, 1, size_x, size_z),
            vm(2, size_y, size_z),
            vm(NSWEEP, 2, 3, size_x, size_z),
            vm(NSWEEP, 2, size_y, size_z),
            vm(NSWEEP, 2, 3, size_x, size_z),
            vm(NSWEEP, 2, size_y, size_z),
            pltpu.VMEM((3, size_x * size_y, slots), jnp.bfloat16),
            pltpu.VMEM((tiles, LANES), jnp.int32),
            vm(count, 16, LANES),
            vm(count, 16, LANES),
            dma((5,)),
            dma((4,)),
            dma((count,)),
            dma((count,)),
            dma((count,)),
            dma((count,)),
            dma((NSWEEP + 1, 6)),
            dma((NSWEEP + 1, 6)),
        ],
        compiler_params=pltpu.CompilerParams(collective_id=0, has_side_effects=True, vmem_limit_bytes=28 << 20),
        name="flow",
    )(*(pltpu.with_memory_space_constraint(x, pltpu.HBM) for x in (tri_geom, send_index, near_index, return_cell, velocity)))
    whole = pl.BlockSpec(memory_space=pltpu.VMEM)
    return pl.pallas_call(
        finish_kernel,
        out_shape=(f32(*velocity.shape), f32(*near_index.shape), f32(9, tri_dev)),
        in_specs=[anywhere, anywhere, whole, whole],
        out_specs=(anywhere,) * 3,
        scratch_shapes=[vm(9, tri_dev), dma((3,))],
        compiler_params=pltpu.CompilerParams(vmem_limit_bytes=8 << 20),
        name="finish",
    )(*left)


def solution(mesh):
    placed = (
        P(None, ("gx", "gy", "gz")),
        P(("gx", "gy", "gz"), None),
        P("gx", "gy", "gz"),
        P(None, ("gx", "gy", "gz")),
        P(None, "gx", "gy", "gz"),
    )
    return jax.shard_map(
        per_device,
        mesh=mesh,
        in_specs=placed,
        out_specs=(P(None, "gx", "gy", "gz"), P("gx", "gy", "gz"), P(None, ("gx", "gy", "gz"))),
        check_vma=False,
    )
```

profile of v0, /device:TPU:0, one launch (start us, length us, event | category | flops | bytes accessed | tf_op | source)
XLA Modules:
  0.0 40.7 jit_solution(17392413890839981865)
XLA Ops:
  0.6 39.1 %flow.1 = (f32[3,8,32,128]{3,2,1,0:T(8,128)S(1)}, f32[8,32,128]{2,1,0:T(8,128)S(1)}, f32[8,16,128]{2,1,0:T(8,128)S(1)}, s32[8,128]{1,0:T(8,128)S(1)}) custom-call(f32[10,1024]{1,0:T(8,128)} %tri_hbm.1, s32[8,128]{1,0:T(8,128)} %send_hbm.1, s32[8,32,128]{2,1,0:T(8,128)} %near_hbm.1, s32[3,1024]{1,0:T(4,128)} %cell_hbm.1, f32[3,8,32,128]{3,2,1,0:T(8,128)} %vel_hbm.1), custom_call_target="tpu_custom_call" | custom-call | tf_op jit(solution)/shard_map/flow/pallas_call | solution.py:562
  39.8 0.9 %finish.1 = (f32[3,8,32,128]{3,2,1,0:T(8,128)}, f32[8,32,128]{2,1,0:T(8,128)}, f32[9,1024]{1,0:T(8,128)}) custom-call(f32[3,8,32,128]{3,2,1,0:T(8,128)S(1)} %get-tuple-element.7.vel_hbm, f32[8,32,128]{2,1,0:T(8,128)S(1)} %get-tuple-element.8.ind_hbm, f32[8,16,128]{2,1,0:T(8,128)S(1)} %get-tuple-element.9.back_ref, s32[8,128]{1,0:T(8,128)S(1)} %get-tuple-element.10.inv_ref), custom_call_target="tpu_custom_call" | custom-call | tf_op jit(solution)/shard_map/finish/pallas_call | solution.py:611
where the time goes:
time: 40.8 us; the launch traced here: 40.7 us
  Pallas kernels  40 us (98%)
  between operations  0.64 us (2%)
    pallas_call x1, Pallas kernels, per_device(): pl.pallas_call(flow_kernel, out_shape=(f32(*velocity.shape), f32(*near_in...  39.1 us
    pallas_call x1, Pallas kernels, per_device(): pl.pallas_call(finish_kernel, out_shape=(f32(*velocity.shape), f32(*near_...  0.89 us

commit v1 on v0

--- a/solution.py
+++ b/solution.py
@@ -42,7 +42,7 @@
     return init
 
 
-UN_NEAR, UN_SWEEP, UN_FIRST, UN_FORCE, UN_INV = 2, 3, 4, 4, 4
+UN_NEAR, UN_SWEEP, UN_FIRST, UN_FORCE, UN_INV = 2, 3, 4, 3, 4
 
 
 def lane_pick(source, lane):
@@ -97,10 +97,8 @@
 
 
 def pack_lanes(plane, p, packed):
-    here = iota(plane.shape, 1) == p
-    low = jnp.where(here, pltpu.roll(plane, p, 1), packed[0])
-    high = jnp.where(here, pltpu.roll(plane, p + 1, 1), packed[1])
-    return (low, high)
+    here = (iota(plane.shape, 1) >> 1) == p
+    return jnp.where(here, pltpu.roll(plane, 2 * p + 1, 1), packed)
 
 
 def pack_rows(plane, c, x, row_ref):
@@ -109,7 +107,20 @@
     row_ref[1, c, pl.ds(x, 1), :] = plane[last : last + 1]
 
 
-def around(field_ref, row_ref, lane_ref, c, x, p):
+def pack_faces(planes, x, row_ref, packed):
+    size_x = row_ref.shape[2]
+    for c, plane in enumerate(planes):
+        pack_rows(plane, c, x, row_ref)
+        packed = pack_lanes(plane, c * size_x + x, packed)
+    return packed
+
+
+def mix_lanes(halo_ref, mix_ref):
+    even = (iota(mix_ref.shape, 1) & 1) == 0
+    mix_ref[...] = jnp.where(even, halo_ref[0], halo_ref[1])
+
+
+def around(field_ref, row_ref, mix_ref, c, x, p):
     size_y, size_z = field_ref.shape[2:]
     row, lane = iota((size_y, size_z), 0), iota((size_y, size_z), 1)
     mid = field_ref[c, x + 1]
@@ -123,51 +134,46 @@
         jnp.broadcast_to(row_ref[1, c, pl.ds(x, 1), :], mid.shape),
         pltpu.roll(mid, size_y - 1, 0),
     )
-    low_z = jnp.where(
-        lane == 0, pltpu.roll(lane_ref[0], (size_z - p) % size_z, 1), pltpu.roll(mid, 1, 1)
-    )
-    high_z = jnp.where(
-        lane == size_z - 1,
-        pltpu.roll(lane_ref[1], size_z - 1 - p, 1),
-        pltpu.roll(mid, size_z - 1, 1),
-    )
+    ends = pltpu.roll(mix_ref[...], size_z - 1 - 2 * p, 1)
+    low_z = pltpu.roll(jnp.where(lane == size_z - 1, ends, mid), 1, 1)
+    high_z = pltpu.roll(jnp.where(lane == 0, ends, mid), size_z - 1, 1)
     return mid, field_ref[c, x], field_ref[c, x + 2], low_y, high_y, low_z, high_z
 
 
-def nearest(tab_ref, near_ref, ind_ref, ten_ref, row_ref, lane_ref):
-    size_x, size_y, size_z = near_ref.shape
-    pos_y = iota((size_y, size_z), 0).astype(jnp.float32) + 0.5
-    pos_z = iota((size_y, size_z), 1).astype(jnp.float32) + 0.5
-    zero = jnp.zeros((size_y, size_z), jnp.float32)
-
-    def plane(x, packed):
-        index = near_ref[x]
-        lane, owner = index & (LANES - 1), index >> 7
-
-        def inner(j, found):
-            here = owner == j
-            return tuple(
-                jnp.where(
-                    here,
-                    lane_pick(
-                        jnp.broadcast_to(tab_ref[f, pl.ds(j, 1), :], (size_y, size_z)), lane
-                    ),
-                    found[f],
-                )
-                for f in range(5)
+def lookup(tab_ref, index):
+    lane, owner = index & (LANES - 1), index >> 7
+
+    def inner(j, found):
+        here = owner == j
+        return tuple(
+            jnp.where(
+                here,
+                lane_pick(jnp.broadcast_to(tab_ref[f, pl.ds(j, 1), :], index.shape), lane),
+                found[f],
             )
-
-        nx, ny, nz, offset, tension = loop(tab_ref.shape[1], inner, (zero,) * 5)
-        pos_x = jnp.asarray(x).astype(jnp.float32) + 0.5
+            for f in range(5)
+        )
+
+    zero = jnp.zeros(index.shape, jnp.float32)
+    return loop(tab_ref.shape[1], inner, (zero,) * 5)
+
+
+def nearest_plane(tab_ref, near_ref, ind_ref, ten_ref, x):
+    size_y, size_z = near_ref.shape[1:]
+    tall = 8 if tab_ref.shape[1] <= 8 else size_y
+    pos_x = jnp.asarray(x).astype(jnp.float32) + 0.5
+    pos_z = iota((tall, size_z), 1).astype(jnp.float32) + 0.5
+    parts = []
+    for r in range(0, size_y, tall):
+        here = slice(r, r + tall)
+        nx, ny, nz, offset, tension = lookup(tab_ref, near_ref[x, here, :])
+        pos_y = iota((tall, size_z), 0).astype(jnp.float32) + (r + 0.5)
         distance = nx * pos_x + ny * pos_y + nz * pos_z + offset
         indicator = 0.5 * (1.0 + jnp.tanh(distance / smear_width))
-        ind_ref[0, x + 1] = indicator
-        ten_ref[x] = tension
-        pack_rows(indicator, 0, x, row_ref)
-        return pack_lanes(indicator, x, packed)
-
-    packed = span(0, size_x, UN_NEAR, plane, (zero, zero))
-    lane_ref[0], lane_ref[1] = packed
+        ind_ref[0, x + 1, here, :] = indicator
+        ten_ref[x, here, :] = tension
+        parts.append(indicator)
+    return jnp.concatenate(parts, axis=0)
 
 
 def material(ind_ref, ten_ref, diff_ref):
@@ -183,29 +189,22 @@
     span(0, ten_ref.shape[0], UN_FORCE, plane, 0)
 
 
-def forces(ind_ref, row_ref, lane_ref, ten_ref, force_ref):
-    def plane(x, carry):
-        near = around(ind_ref, row_ref, lane_ref, 0, x, x)
-        for a in range(3):
-            force_ref[a, x] = ten_ref[x] * (near[2 * a + 2] - near[2 * a + 1])
-        return carry
-
-    span(0, ten_ref.shape[0], UN_FORCE, plane, 0)
-
-
-def advance(old_ref, row_ref, lane_ref, diff_ref, force_ref, new_ref, x, packed, new_rows):
+def forces(ind_ref, row_ref, mix_ref, ten_ref, force_ref, x):
+    near = around(ind_ref, row_ref, mix_ref, 0, x, x)
+    for a in range(3):
+        force_ref[a, x] = ten_ref[x] * (near[2 * a + 2] - near[2 * a + 1])
+
+
+def advance(old_ref, row_ref, mix_ref, diff_ref, force_ref, new_ref, x):
     size_x = diff_ref.shape[0]
     diffusion = diff_ref[x]
+    planes = []
     for c in range(3):
-        p = c * size_x + x
-        mid, *near = around(old_ref, row_ref, lane_ref, c, x, p)
+        mid, *near = around(old_ref, row_ref, mix_ref, c, x, c * size_x + x)
         laplace = near[0] + near[1] + near[2] + near[3] + near[4] + near[5] - 6.0 * mid
-        new = mid + (diffusion * laplace + force_ref[c, x])
-        new_ref[c, x + 1] = new
-        if new_rows is not None:
-            pack_rows(new, c, x, new_rows)
-            packed = pack_lanes(new, p, packed)
-    return packed
+        planes.append(mid + (diffusion * laplace + force_ref[c, x]))
+        new_ref[c, x + 1] = planes[-1]
+    return planes
 
 
 def row_onehot(cell_ref, hot_ref):
@@ -222,7 +221,7 @@
     lax.fori_loop(0, slots // LANES, each, 0)
 
 
-def sample_field(vel_ref, cell_ref, hot_ref, out_ref, send):
+def sample_field(vel_ref, cell_ref, hot_ref, out_ref, send, first, step):
     rows, slots = hot_ref.shape[1:]
     size_x = vel_ref.shape[1] - 2
     parts = [vel_ref[c, 1 : size_x + 1].reshape(rows, LANES).T for c in range(3)]
@@ -230,8 +229,10 @@
     high = field.astype(jnp.bfloat16)
     low = (field - high.astype(jnp.float32)).astype(jnp.bfloat16)
     width = 256
-
-    def each(i, carry):
+    turns = slots // width
+
+    def each(k, carry):
+        i = (first + k * step + turns) % turns
         here = pl.ds(pl.multiple_of(i * width, width), width)
         for v in range(3):
             hot = hot_ref[v, :, here]
@@ -250,7 +251,7 @@
             send(i * (width // LANES) + k)
         return carry
 
-    lax.fori_loop(0, slots // width, each, 0)
+    lax.fori_loop(0, turns, each, 0)
 
 
 def invert(send_ref, inv_ref):
@@ -330,6 +331,7 @@
     lanes_ref,
     row_halo,
     lane_halo,
+    mix_ref,
     hot_ref,
     inv_ref,
     sample_ref,
@@ -404,8 +406,8 @@
             ("gx", -1, field.at[:, 1], field.at[:, size_x + 1]),
             ("gy", 1, rows.at[1], halo_rows.at[0]),
             ("gy", -1, rows.at[0], halo_rows.at[1]),
-            ("gz", 1, lanes.at[1], halo_lanes.at[0]),
-            ("gz", -1, lanes.at[0], halo_lanes.at[1]),
+            ("gz", 1, lanes, halo_lanes.at[0]),
+            ("gz", -1, lanes, halo_lanes.at[1]),
         )
         return [
             remote(src, dst, face_send.at[n, i], face_recv.at[n, i], beside(axis, step))
@@ -443,24 +445,26 @@
     peers(lambda d: there(me, d).start())
     arrived_ref[me] = out_ref[me]
 
+    def start_x(copies):
+        lowest = at["gx"] == 0
+        pl.when(lowest)(lambda: copies[1].start())
+        copies[0].start()
+        pl.when(jnp.logical_not(lowest))(lambda: copies[1].start())
+
+    edges = sorted({0, size_x - 1})
+    zero = jnp.zeros(extent[1:], jnp.float32)
+
+    def first_faces(x, packed):
+        planes = [state_ref[0, c, x + 1] for c in range(3)]
+        return pack_faces(planes, x, rows_ref.at[0], packed)
+
     loads[2].wait()
-    for copy in rounds[0][:2]:
-        copy.start()
-    zero = jnp.zeros(extent[1:], jnp.float32)
-
-    def first_faces(x, packed):
-        for c in range(3):
-            plane = state_ref[0, c, x + 1]
-            pack_rows(plane, c, x, rows_ref.at[0])
-            packed = pack_lanes(plane, c * size_x + x, packed)
-        return packed
-
-    packed = span(0, size_x, UN_FIRST, first_faces, (zero, zero))
-    lanes_ref[0, 0], lanes_ref[0, 1] = packed
+    lanes_ref[0] = span(0, size_x, UN_FIRST, first_faces, zero)
+    loads[4].wait()
+    row_onehot(cell_ref, hot_ref)
+    start_x(rounds[0][:2])
     for copy in rounds[0][2:]:
         copy.start()
-    loads[4].wait()
-    row_onehot(cell_ref, hot_ref)
     invert(send_ref, inv_ref)
     put_inv = pltpu.make_async_copy(inv_ref, inv_out, out_sem.at[3])
     put_inv.start()
@@ -468,41 +472,69 @@
     peers(lambda d: there(d, me).wait_recv())
     origin = [(at[a] * n).astype(jnp.float32) for a, n in zip(AXES, extent)]
     local_table(arrived_ref, tab_ref, origin)
-    nearest(tab_ref, near_ref, ind_ref, ten_ref, ind_rows, ind_lanes)
-    for copy in ind_round:
+
+    def near_plane(x):
+        return nearest_plane(tab_ref, near_ref, ind_ref, ten_ref, x)
+
+    def near_middle(x, packed):
+        return pack_faces([near_plane(x)], x, ind_rows, packed)
+
+    planes = [near_plane(x) for x in edges]
+    start_x(ind_round[:2])
+    packed = zero
+    for x, plane in zip(edges, planes):
+        packed = pack_faces([plane], x, ind_rows, packed)
+    ind_lanes[...] = span(1, size_x - 1, UN_NEAR, near_middle, packed)
+    for copy in ind_round[2:]:
         copy.start()
     put_ind = pltpu.make_async_copy(ind_ref.at[0, 1 : size_x + 1], ind_out, out_sem.at[0])
     put_ind.start()
     material(ind_ref, ten_ref, diff_ref)
-    for copy in ind_round:
+
+    def force_plane(x, carry):
+        forces(ind_ref, ind_row_halo, mix_ref.at[NSWEEP], ten_ref, force_ref, x)
+        return carry
+
+    for copy in ind_round[2:]:
         copy.wait_recv()
-    forces(ind_ref, ind_row_halo, ind_lane_halo, ten_ref, force_ref)
+    mix_lanes(ind_lane_halo, mix_ref.at[NSWEEP])
+    span(1, size_x - 1, UN_FORCE, force_plane, 0)
 
     for n in range(NSWEEP):
         last = n == NSWEEP - 1
-        for copy in rounds[n]:
-            copy.wait_recv()
-
-        def plane(x, packed):
+
+        def plane(x):
             return advance(
                 state_ref.at[n],
                 row_halo.at[n],
-                lane_halo.at[n],
+                mix_ref.at[n],
                 diff_ref,
                 force_ref,
                 state_ref.at[n + 1],
                 x,
-                packed,
-                None if last else rows_ref.at[n + 1],
             )
 
-        packed = plane(size_x - 1, plane(0, (zero, zero)))
+        def middle(x, packed):
+            planes = plane(x)
+            return packed if last else pack_faces(planes, x, rows_ref.at[n + 1], packed)
+
+        for copy in rounds[n][2:]:
+            copy.wait_recv()
+        mix_lanes(lane_halo.at[n], mix_ref.at[n])
+        packed = span(1, size_x - 1, UN_SWEEP, middle, zero)
+        if n == 0:
+            for copy in ind_round[:2]:
+                copy.wait_recv()
+            for x in edges:
+                force_plane(x, 0)
+        for copy in rounds[n][:2]:
+            copy.wait_recv()
+        planes = [plane(x) for x in edges]
         if not last:
-            for copy in rounds[n + 1][:2]:
-                copy.start()
-        packed = span(1, size_x - 1, UN_SWEEP, plane, packed)
-        if not last:
-            lanes_ref[n + 1, 0], lanes_ref[n + 1, 1] = packed
+            start_x(rounds[n + 1][:2])
+            for x, group in zip(edges, planes):
+                packed = pack_faces(group, x, rows_ref.at[n + 1], packed)
+            lanes_ref[n + 1] = packed
             for copy in rounds[n + 1][2:]:
                 copy.start()
     put_vel = pltpu.make_async_copy(
@@ -515,7 +547,12 @@
         def _():
             back(me, d).start()
 
-    sample_field(state_ref.at[NSWEEP], cell_ref, hot_ref, sample_ref, send_back)
+    share = sample_ref.shape[0] // 2 // size["gx"]
+    upper = (2 * at["gx"]) // size["gx"]
+    first = (at["gx"] + upper) * share - (1 - upper)
+    sample_field(
+        state_ref.at[NSWEEP], cell_ref, hot_ref, sample_ref, send_back, first, 2 * upper - 1
+    )
     back_ref[me] = sample_ref[me]
     peers(lambda d: back(d, me).wait_recv())
     put_back = pltpu.make_async_copy(back_ref, back_out, out_sem.at[2])
@@ -584,13 +621,14 @@
             vm(3, size_x, size_y, size_z),
             vm(NSWEEP + 1, 3, size_x + 2, size_y, size_z),
             vm(2, 1, size_x, size_z),
-            vm(2, size_y, size_z),
+            vm(size_y, size_z),
             vm(2, 1, size_x, size_z),
             vm(2, size_y, size_z),
             vm(NSWEEP, 2, 3, size_x, size_z),
-            vm(NSWEEP, 2, size_y, size_z),
+            vm(NSWEEP, size_y, size_z),
             vm(NSWEEP, 2, 3, size_x, size_z),
             vm(NSWEEP, 2, size_y, size_z),
+            vm(NSWEEP + 1, size_y, size_z),
             pltpu.VMEM((3, size_x * size_y, slots), jnp.bfloat16),
             pltpu.VMEM((tiles, LANES), jnp.int32),
             vm(count, 16, LANES),

time: 40.8 us -> 37.1 us (0.909)
  Pallas kernels: 40 us -> 36.3 us
    pallas_call x1, Pallas kernels: 39.1 us -> 35.4 us  [per_device(): pl.pallas_call(flow_kernel, out_shape=(f32(*velocity.shape), f32(*near_in...]
where the time goes in v1:
time: 37.1 us; the launch traced here: 37 us
  Pallas kernels  36.3 us (98%)
  between operations  0.64 us (2%)
    pallas_call x1, Pallas kernels, per_device(): pl.pallas_call(flow_kernel, out_shape=(f32(*velocity.shape), f32(*near_in...  35.4 us
    pallas_call x1, Pallas kernels, per_device(): pl.pallas_call(finish_kernel, out_shape=(f32(*velocity.shape), f32(*near_...  0.89 us

profile of v1, /device:TPU:0, one launch (start us, length us, event | category | flops | bytes accessed | tf_op | source)
XLA Modules:
  0.0 37.0 jit_solution(6242544046354238343)
XLA Ops:
  0.6 35.4 %flow.1 = (f32[3,8,32,128]{3,2,1,0:T(8,128)S(1)}, f32[8,32,128]{2,1,0:T(8,128)S(1)}, f32[8,16,128]{2,1,0:T(8,128)S(1)}, s32[8,128]{1,0:T(8,128)S(1)}) custom-call(f32[10,1024]{1,0:T(8,128)} %tri_hbm.1, s32[8,128]{1,0:T(8,128)} %send_hbm.1, s32[8,32,128]{2,1,0:T(8,128)} %near_hbm.1, s32[3,1024]{1,0:T(4,128)} %cell_hbm.1, f32[3,8,32,128]{3,2,1,0:T(8,128)} %vel_hbm.1), custom_call_target="tpu_custom_call" | custom-call | tf_op jit(solution)/shard_map/flow/pallas_call | solution.py:599
  36.1 0.9 %finish.1 = (f32[3,8,32,128]{3,2,1,0:T(8,128)}, f32[8,32,128]{2,1,0:T(8,128)}, f32[9,1024]{1,0:T(8,128)}) custom-call(f32[3,8,32,128]{3,2,1,0:T(8,128)S(1)} %get-tuple-element.7.vel_hbm, f32[8,32,128]{2,1,0:T(8,128)S(1)} %get-tuple-element.8.ind_hbm, f32[8,16,128]{2,1,0:T(8,128)S(1)} %get-tuple-element.9.back_ref, s32[8,128]{1,0:T(8,128)S(1)} %get-tuple-element.10.inv_ref), custom_call_target="tpu_custom_call" | custom-call | tf_op jit(solution)/shard_map/finish/pallas_call | solution.py:649

commit v2 on v1

--- a/solution.py
+++ b/solution.py
@@ -158,22 +158,37 @@
     return loop(tab_ref.shape[1], inner, (zero,) * 5)
 
 
+def indicate(tab_ref, index, position):
+    nx, ny, nz, offset, tension = lookup(tab_ref, index)
+    pos_x, pos_y, pos_z = (jnp.asarray(p).astype(jnp.float32) + 0.5 for p in position)
+    distance = nx * pos_x + ny * pos_y + nz * pos_z + offset
+    return 0.5 * (1.0 + jnp.tanh(distance / smear_width)), tension
+
+
 def nearest_plane(tab_ref, near_ref, ind_ref, ten_ref, x):
     size_y, size_z = near_ref.shape[1:]
     tall = 8 if tab_ref.shape[1] <= 8 else size_y
-    pos_x = jnp.asarray(x).astype(jnp.float32) + 0.5
-    pos_z = iota((tall, size_z), 1).astype(jnp.float32) + 0.5
-    parts = []
     for r in range(0, size_y, tall):
         here = slice(r, r + tall)
-        nx, ny, nz, offset, tension = lookup(tab_ref, near_ref[x, here, :])
-        pos_y = iota((tall, size_z), 0).astype(jnp.float32) + (r + 0.5)
-        distance = nx * pos_x + ny * pos_y + nz * pos_z + offset
-        indicator = 0.5 * (1.0 + jnp.tanh(distance / smear_width))
+        position = (x, iota((tall, size_z), 0) + r, iota((tall, size_z), 1))
+        indicator, tension = indicate(tab_ref, near_ref[x, here, :], position)
         ind_ref[0, x + 1, here, :] = indicator
         ten_ref[x, here, :] = tension
-        parts.append(indicator)
-    return jnp.concatenate(parts, axis=0)
+
+
+def nearest_faces(tab_ref, near_rows, near_lanes, row_ref, lane_ref):
+    size_x, size_z = near_rows.shape[2:]
+    size_y = near_lanes.shape[0]
+    shape = (size_x, size_z)
+    for side, y in ((0, 0), (1, size_y - 1)):
+        position = (iota(shape, 0), y, iota(shape, 1))
+        row_ref[side, 0] = indicate(tab_ref, near_rows[side, 0], position)[0]
+    tall = 8 if tab_ref.shape[1] <= 8 else size_y
+    for r in range(0, size_y, tall):
+        here = slice(r, r + tall)
+        lane = iota((tall, size_z), 1)
+        position = (lane >> 1, iota((tall, size_z), 0) + r, (1 - (lane & 1)) * (size_z - 1))
+        lane_ref[here, :] = indicate(tab_ref, near_lanes[here, :], position)[0]
 
 
 def material(ind_ref, ten_ref, diff_ref):
@@ -195,14 +210,27 @@
         force_ref[a, x] = ten_ref[x] * (near[2 * a + 2] - near[2 * a + 1])
 
 
+def laplacian(old_ref, row_ref, mix_ref, c, x, p):
+    mid, *near = around(old_ref, row_ref, mix_ref, c, x, p)
+    return mid, near[0] + near[1] + near[2] + near[3] + near[4] + near[5] - 6.0 * mid
+
+
 def advance(old_ref, row_ref, mix_ref, diff_ref, force_ref, new_ref, x):
     size_x = diff_ref.shape[0]
     diffusion = diff_ref[x]
     planes = []
     for c in range(3):
-        mid, *near = around(old_ref, row_ref, mix_ref, c, x, c * size_x + x)
-        laplace = near[0] + near[1] + near[2] + near[3] + near[4] + near[5] - 6.0 * mid
+        mid, laplace = laplacian(old_ref, row_ref, mix_ref, c, x, c * size_x + x)
         planes.append(mid + (diffusion * laplace + force_ref[c, x]))
+        new_ref[c, x + 1] = planes[-1]
+    return planes
+
+
+def advance_first(old_ref, diff_ref, force_ref, new_ref, x):
+    diffusion = diff_ref[x]
+    planes = []
+    for c in range(3):
+        planes.append(old_ref[c, x + 1] + (diffusion * new_ref[c, x + 1] + force_ref[c, x]))
         new_ref[c, x + 1] = planes[-1]
     return planes
 
@@ -275,19 +303,13 @@
     span(0, send_ref.shape[0], UN_INV if send_ref.shape[0] <= 8 else 1, each, 0)
 
 
-def place_back(inv_ref, back_ref, out_ref):
+def place_back(inv_ref, back_ref, d, out_ref):
     tall = back_ref.shape[1]
 
     def each(t, carry):
         index = jnp.broadcast_to(inv_ref[pl.ds(t, 1), :], (tall, LANES))
         lane, dest = index & (LANES - 1), index >> 7
-
-        def inner(d, found):
-            return jnp.where(dest == d, lane_pick(back_ref[d], lane), found)
-
-        found = loop(back_ref.shape[0], inner, jnp.zeros((tall, LANES), jnp.float32))
-        start = t * LANES if isinstance(t, int) else pl.multiple_of(t * LANES, LANES)
-        out_ref[:, pl.ds(start, LANES)] = found[:9]
+        out_ref[t] = jnp.where(dest == d, lane_pick(back_ref[d], lane), out_ref[t])
         return carry
 
     loop(inv_ref.shape[0], each, 0)
@@ -308,8 +330,7 @@
     vel_hbm,
     vel_out,
     ind_out,
-    back_out,
-    inv_out,
+    vert_out,
     tri_ref,
     send_ref,
     near_ref,
@@ -332,10 +353,13 @@
     row_halo,
     lane_halo,
     mix_ref,
+    near_rows,
+    near_lanes,
     hot_ref,
     inv_ref,
     sample_ref,
     back_ref,
+    vert_ref,
     in_sem,
     out_sem,
     there_send,
@@ -402,8 +426,6 @@
 
     def faces(n, field, rows, lanes, halo_rows, halo_lanes):
         pairs = (
-            ("gx", 1, field.at[:, size_x], field.at[:, 0]),
-            ("gx", -1, field.at[:, 1], field.at[:, size_x + 1]),
             ("gy", 1, rows.at[1], halo_rows.at[0]),
             ("gy", -1, rows.at[0], halo_rows.at[1]),
             ("gz", 1, lanes, halo_lanes.at[0]),
@@ -411,7 +433,7 @@
         )
         return [
             remote(src, dst, face_send.at[n, i], face_recv.at[n, i], beside(axis, step))
-            for i, (axis, step, src, dst) in enumerate(pairs)
+            for i, (axis, step, src, dst) in enumerate(pairs, 2)
         ]
 
     rounds = [
@@ -427,6 +449,16 @@
     ]
     ind_round = faces(NSWEEP, ind_ref, ind_rows, ind_lanes, ind_row_halo, ind_lane_halo)
 
+    def x_face(n, up):
+        field = ind_ref if n == NSWEEP else state_ref.at[n]
+        return remote(
+            field.at[:, 1 + up * (size_x - 1)],
+            field.at[:, (1 - up) * (size_x + 1)],
+            face_send.at[n, 1 - up],
+            face_recv.at[n, 1 - up],
+            beside("gx", 2 * up - 1),
+        )
+
     def there(src, dst):
         return remote(
             out_ref.at[dst], arrived_ref.at[src], there_send.at[dst], there_recv.at[src], other(dst)
@@ -445,65 +477,72 @@
     peers(lambda d: there(me, d).start())
     arrived_ref[me] = out_ref[me]
 
-    def start_x(copies):
-        lowest = at["gx"] == 0
-        pl.when(lowest)(lambda: copies[1].start())
-        copies[0].start()
-        pl.when(jnp.logical_not(lowest))(lambda: copies[1].start())
-
-    edges = sorted({0, size_x - 1})
+    lowest = (size["gx"] - 1 - at["gx"]) // (size["gx"] - 1)
+    sides = ((1 - lowest), lowest)
     zero = jnp.zeros(extent[1:], jnp.float32)
 
     def first_faces(x, packed):
         planes = [state_ref[0, c, x + 1] for c in range(3)]
         return pack_faces(planes, x, rows_ref.at[0], packed)
+
+    def near_faces(x, packed):
+        return pack_faces([near_ref[x]], x, near_rows, packed)
 
     loads[2].wait()
     lanes_ref[0] = span(0, size_x, UN_FIRST, first_faces, zero)
     loads[4].wait()
     row_onehot(cell_ref, hot_ref)
-    start_x(rounds[0][:2])
-    for copy in rounds[0][2:]:
+    for up in (0, 1):
+        x_face(0, up).start()
+    for copy in rounds[0]:
         copy.start()
+    loads[3].wait()
+    near_lanes[...] = span(0, size_x, UN_FIRST, near_faces, jnp.zeros(extent[1:], jnp.int32))
     invert(send_ref, inv_ref)
-    put_inv = pltpu.make_async_copy(inv_ref, inv_out, out_sem.at[3])
-    put_inv.start()
-    loads[3].wait()
+    vert_ref[...] = jnp.zeros(vert_ref.shape, jnp.float32)
     peers(lambda d: there(d, me).wait_recv())
     origin = [(at[a] * n).astype(jnp.float32) for a, n in zip(AXES, extent)]
     local_table(arrived_ref, tab_ref, origin)
 
-    def near_plane(x):
-        return nearest_plane(tab_ref, near_ref, ind_ref, ten_ref, x)
-
-    def near_middle(x, packed):
-        return pack_faces([near_plane(x)], x, ind_rows, packed)
-
-    planes = [near_plane(x) for x in edges]
-    start_x(ind_round[:2])
-    packed = zero
-    for x, plane in zip(edges, planes):
-        packed = pack_faces([plane], x, ind_rows, packed)
-    ind_lanes[...] = span(1, size_x - 1, UN_NEAR, near_middle, packed)
-    for copy in ind_round[2:]:
+    def near_plane(x, carry):
+        nearest_plane(tab_ref, near_ref, ind_ref, ten_ref, x)
+        return carry
+
+    for up in sides:
+        near_plane(up * (size_x - 1), 0)
+        x_face(NSWEEP, up).start()
+    nearest_faces(tab_ref, near_rows, near_lanes, ind_rows, ind_lanes)
+    for copy in ind_round:
         copy.start()
+    span(1, size_x - 1, UN_NEAR, near_plane, 0)
     put_ind = pltpu.make_async_copy(ind_ref.at[0, 1 : size_x + 1], ind_out, out_sem.at[0])
     put_ind.start()
     material(ind_ref, ten_ref, diff_ref)
-
-    def force_plane(x, carry):
-        forces(ind_ref, ind_row_halo, mix_ref.at[NSWEEP], ten_ref, force_ref, x)
+    for up in (0, 1):
+        x_face(0, up).wait_recv()
+    for copy in rounds[0]:
+        copy.wait_recv()
+    mix_lanes(lane_halo.at[0], mix_ref.at[0])
+
+    def first_laplacian(x, carry):
+        for c in range(3):
+            state_ref[1, c, x + 1] = laplacian(
+                state_ref.at[0], row_halo.at[0], mix_ref.at[0], c, x, c * size_x + x
+            )[1]
         return carry
 
-    for copy in ind_round[2:]:
-        copy.wait_recv()
-    mix_lanes(ind_lane_halo, mix_ref.at[NSWEEP])
-    span(1, size_x - 1, UN_FORCE, force_plane, 0)
+    span(0, size_x, UN_FIRST, first_laplacian, 0)
 
     for n in range(NSWEEP):
         last = n == NSWEEP - 1
+        faces_in = ind_round if n == 0 else rounds[n]
 
         def plane(x):
+            if n == 0:
+                forces(ind_ref, ind_row_halo, mix_ref.at[NSWEEP], ten_ref, force_ref, x)
+                return advance_first(
+                    state_ref.at[0], diff_ref, force_ref, state_ref.at[1], x
+                )
             return advance(
                 state_ref.at[n],
                 row_halo.at[n],
@@ -518,24 +557,24 @@
             planes = plane(x)
             return packed if last else pack_faces(planes, x, rows_ref.at[n + 1], packed)
 
-        for copy in rounds[n][2:]:
+        for copy in faces_in:
             copy.wait_recv()
-        mix_lanes(lane_halo.at[n], mix_ref.at[n])
+        if n == 0:
+            mix_lanes(ind_lane_halo, mix_ref.at[NSWEEP])
+        else:
+            mix_lanes(lane_halo.at[n], mix_ref.at[n])
         packed = span(1, size_x - 1, UN_SWEEP, middle, zero)
-        if n == 0:
-            for copy in ind_round[:2]:
-                copy.wait_recv()
-            for x in edges:
-                force_plane(x, 0)
-        for copy in rounds[n][:2]:
-            copy.wait_recv()
-        planes = [plane(x) for x in edges]
+        edges = []
+        for up in reversed(sides):
+            x_face(n if n else NSWEEP, 1 - up).wait_recv()
+            edges.append((up * (size_x - 1), plane(up * (size_x - 1))))
+            if not last:
+                x_face(n + 1, up).start()
         if not last:
-            start_x(rounds[n + 1][:2])
-            for x, group in zip(edges, planes):
-                packed = pack_faces(group, x, rows_ref.at[n + 1], packed)
+            for x, planes in edges:
+                packed = pack_faces(planes, x, rows_ref.at[n + 1], packed)
             lanes_ref[n + 1] = packed
-            for copy in rounds[n + 1][2:]:
+            for copy in rounds[n + 1]:
                 copy.start()
     put_vel = pltpu.make_async_copy(
         state_ref.at[NSWEEP, :, 1 : size_x + 1], vel_out, out_sem.at[1]
@@ -554,32 +593,38 @@
         state_ref.at[NSWEEP], cell_ref, hot_ref, sample_ref, send_back, first, 2 * upper - 1
     )
     back_ref[me] = sample_ref[me]
-    peers(lambda d: back(d, me).wait_recv())
-    put_back = pltpu.make_async_copy(back_ref, back_out, out_sem.at[2])
-    put_back.start()
+    place_back(inv_ref, back_ref, me, vert_ref)
+
+    def collect(d):
+        back(d, me).wait_recv()
+        place_back(inv_ref, back_ref, d, vert_ref)
+
+    peers(collect)
+    put_vert = pltpu.make_async_copy(vert_ref, vert_out, out_sem.at[2])
+    put_vert.start()
     peers(lambda d: there(me, d).wait_send())
     peers(lambda d: back(me, d).wait_send())
+    for n in range(NSWEEP + 1):
+        for up in (0, 1):
+            x_face(n, up).wait_send()
     for group in (ind_round, *rounds):
         for copy in group:
             copy.wait_send()
     put_ind.wait()
     put_vel.wait()
-    put_back.wait()
-    put_inv.wait()
-
-
-def finish_kernel(
-    vel_hbm, ind_hbm, back_ref, inv_ref, vel_out, ind_out, vert_out, vert_ref, sem
-):
+    put_vert.wait()
+
+
+def finish_kernel(vel_hbm, ind_hbm, vert_ref, vel_out, ind_out, vert_out, flat_ref, sem):
+    for t in range(vert_ref.shape[0]):
+        flat_ref[:, t * LANES : (t + 1) * LANES] = vert_ref[t, :9]
     give = [
         pltpu.make_async_copy(vel_hbm, vel_out, sem.at[0]),
         pltpu.make_async_copy(ind_hbm, ind_out, sem.at[1]),
-        pltpu.make_async_copy(vert_ref, vert_out, sem.at[2]),
+        pltpu.make_async_copy(flat_ref, vert_out, sem.at[2]),
     ]
-    give[0].start()
-    give[1].start()
-    place_back(inv_ref, back_ref, vert_ref)
-    give[2].start()
+    for copy in give:
+        copy.start()
     for copy in give:
         copy.wait()
 
@@ -601,11 +646,10 @@
         out_shape=(
             f32(*velocity.shape),
             f32(*near_index.shape),
-            f32(count, 16, LANES),
-            jax.ShapeDtypeStruct((tiles, LANES), jnp.int32),
+            f32(tiles, 16, LANES),
         ),
         in_specs=[anywhere] * 5,
-        out_specs=(anywhere,) * 4,
+        out_specs=(anywhere,) * 3,
         scratch_shapes=[
             vm(*tri_geom.shape),
             pltpu.VMEM(send_index.shape, jnp.int32),
@@ -629,12 +673,15 @@
             vm(NSWEEP, 2, 3, size_x, size_z),
             vm(NSWEEP, 2, size_y, size_z),
             vm(NSWEEP + 1, size_y, size_z),
+            pltpu.VMEM((2, 1, size_x, size_z), jnp.int32),
+            pltpu.VMEM((size_y, size_z), jnp.int32),
             pltpu.VMEM((3, size_x * size_y, slots), jnp.bfloat16),
             pltpu.VMEM((tiles, LANES), jnp.int32),
             vm(count, 16, LANES),
             vm(count, 16, LANES),
+            vm(tiles, 16, LANES),
             dma((5,)),
-            dma((4,)),
+            dma((3,)),
             dma((count,)),
             dma((count,)),
             dma((count,)),
@@ -649,7 +696,7 @@
     return pl.pallas_call(
         finish_kernel,
         out_shape=(f32(*velocity.shape), f32(*near_index.shape), f32(9, tri_dev)),
-        in_specs=[anywhere, anywhere, whole, whole],
+        in_specs=[anywhere, anywhere, whole],
         out_specs=(anywhere,) * 3,
         scratch_shapes=[vm(9, tri_dev), dma((3,))],
         compiler_params=pltpu.CompilerParams(vmem_limit_bytes=8 << 20),

time: 37.1 us -> 36.4 us (0.981)
  Pallas kernels: 36.3 us -> 35.6 us
    pallas_call x1, Pallas kernels: 35.4 us -> 34.7 us  [per_device(): pl.pallas_call(flow_kernel, out_shape=(f32(*velocity.shape), f32(*near_in...]
where the time goes in v2:
time: 36.4 us; the launch traced here: 36.2 us
  Pallas kernels  35.6 us (98%)
  between operations  0.64 us (2%)
    pallas_call x1, Pallas kernels, per_device(): pl.pallas_call(flow_kernel, out_shape=(f32(*velocity.shape), f32(*near_in...  34.7 us
    pallas_call x1, Pallas kernels, per_device(): pl.pallas_call(finish_kernel, out_shape=(f32(*velocity.shape), f32(*near_...  0.83 us

profile of v2, /device:TPU:0, one launch (start us, length us, event | category | flops | bytes accessed | tf_op | source)
XLA Modules:
  0.0 36.2 jit_solution(5005889386615032036)
XLA Ops:
  0.6 34.7 %flow.1 = (f32[3,8,32,128]{3,2,1,0:T(8,128)S(1)}, f32[8,32,128]{2,1,0:T(8,128)S(1)}, f32[8,16,128]{2,1,0:T(8,128)S(1)}) custom-call(f32[10,1024]{1,0:T(8,128)} %tri_hbm.1, s32[8,128]{1,0:T(8,128)} %send_hbm.1, s32[8,32,128]{2,1,0:T(8,128)} %near_hbm.1, s32[3,1024]{1,0:T(4,128)} %cell_hbm.1, f32[3,8,32,128]{3,2,1,0:T(8,128)} %vel_hbm.1), custom_call_target="tpu_custom_call" | custom-call | tf_op jit(solution)/shard_map/flow/pallas_call | solution.py:644
  35.4 0.8 %finish.1 = (f32[3,8,32,128]{3,2,1,0:T(8,128)}, f32[8,32,128]{2,1,0:T(8,128)}, f32[9,1024]{1,0:T(8,128)}) custom-call(f32[3,8,32,128]{3,2,1,0:T(8,128)S(1)} %get-tuple-element.6.vel_hbm, f32[8,32,128]{2,1,0:T(8,128)S(1)} %get-tuple-element.7.ind_hbm, f32[8,16,128]{2,1,0:T(8,128)S(1)} %get-tuple-element.8.vert_ref), custom_call_target="tpu_custom_call" | custom-call | tf_op jit(solution)/shard_map/finish/pallas_call | solution.py:696

commit v3 on v2

--- a/solution.py
+++ b/solution.py
@@ -303,13 +303,19 @@
     span(0, send_ref.shape[0], UN_INV if send_ref.shape[0] <= 8 else 1, each, 0)
 
 
-def place_back(inv_ref, back_ref, d, out_ref):
+def place_back(inv_ref, back_ref, out_ref):
     tall = back_ref.shape[1]
 
     def each(t, carry):
         index = jnp.broadcast_to(inv_ref[pl.ds(t, 1), :], (tall, LANES))
         lane, dest = index & (LANES - 1), index >> 7
-        out_ref[t] = jnp.where(dest == d, lane_pick(back_ref[d], lane), out_ref[t])
+
+        def inner(d, found):
+            return jnp.where(dest == d, lane_pick(back_ref[d], lane), found)
+
+        found = loop(back_ref.shape[0], inner, jnp.zeros((tall, LANES), jnp.float32))
+        start = t * LANES if isinstance(t, int) else pl.multiple_of(t * LANES, LANES)
+        out_ref[:, pl.ds(start, LANES)] = found[:9]
         return carry
 
     loop(inv_ref.shape[0], each, 0)
@@ -330,7 +336,8 @@
     vel_hbm,
     vel_out,
     ind_out,
-    vert_out,
+    back_out,
+    inv_out,
     tri_ref,
     send_ref,
     near_ref,
@@ -359,7 +366,6 @@
     inv_ref,
     sample_ref,
     back_ref,
-    vert_ref,
     in_sem,
     out_sem,
     there_send,
@@ -499,7 +505,8 @@
     loads[3].wait()
     near_lanes[...] = span(0, size_x, UN_FIRST, near_faces, jnp.zeros(extent[1:], jnp.int32))
     invert(send_ref, inv_ref)
-    vert_ref[...] = jnp.zeros(vert_ref.shape, jnp.float32)
+    put_inv = pltpu.make_async_copy(inv_ref, inv_out, out_sem.at[3])
+    put_inv.start()
     peers(lambda d: there(d, me).wait_recv())
     origin = [(at[a] * n).astype(jnp.float32) for a, n in zip(AXES, extent)]
     local_table(arrived_ref, tab_ref, origin)
@@ -508,12 +515,13 @@
         nearest_plane(tab_ref, near_ref, ind_ref, ten_ref, x)
         return carry
 
-    for up in sides:
-        near_plane(up * (size_x - 1), 0)
-        x_face(NSWEEP, up).start()
+    near_plane(sides[0] * (size_x - 1), 0)
+    x_face(NSWEEP, sides[0]).start()
     nearest_faces(tab_ref, near_rows, near_lanes, ind_rows, ind_lanes)
     for copy in ind_round:
         copy.start()
+    near_plane(sides[1] * (size_x - 1), 0)
+    x_face(NSWEEP, sides[1]).start()
     span(1, size_x - 1, UN_NEAR, near_plane, 0)
     put_ind = pltpu.make_async_copy(ind_ref.at[0, 1 : size_x + 1], ind_out, out_sem.at[0])
     put_ind.start()
@@ -593,15 +601,9 @@
         state_ref.at[NSWEEP], cell_ref, hot_ref, sample_ref, send_back, first, 2 * upper - 1
     )
     back_ref[me] = sample_ref[me]
-    place_back(inv_ref, back_ref, me, vert_ref)
-
-    def collect(d):
-        back(d, me).wait_recv()
-        place_back(inv_ref, back_ref, d, vert_ref)
-
-    peers(collect)
-    put_vert = pltpu.make_async_copy(vert_ref, vert_out, out_sem.at[2])
-    put_vert.start()
+    peers(lambda d: back(d, me).wait_recv())
+    put_back = pltpu.make_async_copy(back_ref, back_out, out_sem.at[2])
+    put_back.start()
     peers(lambda d: there(me, d).wait_send())
     peers(lambda d: back(me, d).wait_send())
     for n in range(NSWEEP + 1):
@@ -612,19 +614,22 @@
             copy.wait_send()
     put_ind.wait()
     put_vel.wait()
-    put_vert.wait()
-
-
-def finish_kernel(vel_hbm, ind_hbm, vert_ref, vel_out, ind_out, vert_out, flat_ref, sem):
-    for t in range(vert_ref.shape[0]):
-        flat_ref[:, t * LANES : (t + 1) * LANES] = vert_ref[t, :9]
+    put_back.wait()
+    put_inv.wait()
+
+
+def finish_kernel(
+    vel_hbm, ind_hbm, back_ref, inv_ref, vel_out, ind_out, vert_out, vert_ref, sem
+):
     give = [
         pltpu.make_async_copy(vel_hbm, vel_out, sem.at[0]),
         pltpu.make_async_copy(ind_hbm, ind_out, sem.at[1]),
-        pltpu.make_async_copy(flat_ref, vert_out, sem.at[2]),
+        pltpu.make_async_copy(vert_ref, vert_out, sem.at[2]),
     ]
-    for copy in give:
-        copy.start()
+    give[0].start()
+    give[1].start()
+    place_back(inv_ref, back_ref, vert_ref)
+    give[2].start()
     for copy in give:
         copy.wait()
 
@@ -646,10 +651,11 @@
         out_shape=(
             f32(*velocity.shape),
             f32(*near_index.shape),
-            f32(tiles, 16, LANES),
+            f32(count, 16, LANES),
+            jax.ShapeDtypeStruct((tiles, LANES), jnp.int32),
         ),
         in_specs=[anywhere] * 5,
-        out_specs=(anywhere,) * 3,
+        out_specs=(anywhere,) * 4,
         scratch_shapes=[
             vm(*tri_geom.shape),
             pltpu.VMEM(send_index.shape, jnp.int32),
@@ -679,9 +685,8 @@
             pltpu.VMEM((tiles, LANES), jnp.int32),
             vm(count, 16, LANES),
             vm(count, 16, LANES),
-            vm(tiles, 16, LANES),
             dma((5,)),
-            dma((3,)),
+            dma((4,)),
             dma((count,)),
             dma((count,)),
             dma((count,)),
@@ -696,7 +701,7 @@
     return pl.pallas_call(
         finish_kernel,
         out_shape=(f32(*velocity.shape), f32(*near_index.shape), f32(9, tri_dev)),
-        in_specs=[anywhere, anywhere, whole],
+        in_specs=[anywhere, anywhere, whole, whole],
         out_specs=(anywhere,) * 3,
         scratch_shapes=[vm(9, tri_dev), dma((3,))],
         compiler_params=pltpu.CompilerParams(vmem_limit_bytes=8 << 20),

time: 36.4 us -> 35.8 us (0.984)
  Pallas kernels: 35.6 us -> 35 us
    pallas_call x1, Pallas kernels: 34.7 us -> 34.1 us  [per_device(): pl.pallas_call(flow_kernel, out_shape=(f32(*velocity.shape), f32(*near_in...]
where the time goes in v3:
time: 35.8 us; the launch traced here: 35.6 us
  Pallas kernels  35 us (98%)
  between operations  0.64 us (2%)
    pallas_call x1, Pallas kernels, per_device(): pl.pallas_call(flow_kernel, out_shape=(f32(*velocity.shape), f32(*near_in...  34.1 us
    pallas_call x1, Pallas kernels, per_device(): pl.pallas_call(finish_kernel, out_shape=(f32(*velocity.shape), f32(*near_...  0.89 us

profile of v3, /device:TPU:0, one launch (start us, length us, event | category | flops | bytes accessed | tf_op | source)
XLA Modules:
  0.0 35.6 jit_solution(13090712178077158443)
XLA Ops:
  0.6 34.1 %flow.1 = (f32[3,8,32,128]{3,2,1,0:T(8,128)S(1)}, f32[8,32,128]{2,1,0:T(8,128)S(1)}, f32[8,16,128]{2,1,0:T(8,128)S(1)}, s32[8,128]{1,0:T(8,128)S(1)}) custom-call(f32[10,1024]{1,0:T(8,128)} %tri_hbm.1, s32[8,128]{1,0:T(8,128)} %send_hbm.1, s32[8,32,128]{2,1,0:T(8,128)} %near_hbm.1, s32[3,1024]{1,0:T(4,128)} %cell_hbm.1, f32[3,8,32,128]{3,2,1,0:T(8,128)} %vel_hbm.1), custom_call_target="tpu_custom_call" | custom-call | tf_op jit(solution)/shard_map/flow/pallas_call | solution.py:649
  34.7 0.9 %finish.1 = (f32[3,8,32,128]{3,2,1,0:T(8,128)}, f32[8,32,128]{2,1,0:T(8,128)}, f32[9,1024]{1,0:T(8,128)}) custom-call(f32[3,8,32,128]{3,2,1,0:T(8,128)S(1)} %get-tuple-element.7.vel_hbm, f32[8,32,128]{2,1,0:T(8,128)S(1)} %get-tuple-element.8.ind_hbm, f32[8,16,128]{2,1,0:T(8,128)S(1)} %get-tuple-element.9.back_ref, s32[8,128]{1,0:T(8,128)S(1)} %get-tuple-element.10.inv_ref), custom_call_target="tpu_custom_call" | custom-call | tf_op jit(solution)/shard_map/finish/pallas_call | solution.py:701
